TPU v7x, 32 devices: a whole 2x2x4 slice. The times are simulated.
32 devices in a mesh: section: 2 (over x), seq: 16 (over z, y, core).
Axes of the slice: x: 2, y: 2, z: 4, core: 2. Of those that a mesh axis runs over, the one named last changes fastest.
Arguments:
- prev_out: bfloat16 [2, 2048, 1792], P('section', 'seq'), may hold values from -6 to 6
- prev_grad: bfloat16 [2, 2048, 1792], P('section', 'seq'), may hold values from -6 to 6
- saved_in: bfloat16 [2, 2048, 1792], P('section', 'seq'), may hold values from -6 to 6
- seq_mix: bfloat16 [2, 128, 128], P('section'), may hold values from -0.5 to 0.5
- coeffs: float32 [2, 4, 4, 1792], P('section'), may hold values from -1 to 1
- mixer: bfloat16 [2, 1792, 448], P('section'), may hold values from -0.25 to 0.25
Outputs:
- out_fwd: bfloat16 [2, 2048, 1792], P('section', 'seq')
- out_dh: bfloat16 [2, 2048, 1792], P('section', 'seq')
- grad_w: float32 [2, 1792, 448], P('section', 'seq')
- grad_b: float32 [2, 128, 128], P('section')
All inputs are finite; a program needn't handle non-finite values.
Results may differ from a plain program's by a relative error of at most 0.01.
Values may be sent and summed in bfloat16 or wider, within the bound.
No kernel may reach another device: no remote copies, remote signals or barrier semaphores. Data moves between devices by JAX's collectives and lax.ppermute only.
A program may use at most 64 MiB of HBM per device.

v0:
```python
import jax
import jax.numpy as jnp
from jax import lax
from jax.sharding import PartitionSpec as P


def swapped(block, axis, stride):
    count = lax.axis_size(axis)
    route = []
    for low in range(count):
        high = low | 1 << stride
        if high != low and high < count:
            route += [(low, high), (high, low)]
    return lax.ppermute(block, axis, route)


def from_behind(block, axis, distance):
    devices = range(lax.axis_size(axis))
    route = [((i - distance) % len(devices), i) for i in devices]
    return lax.ppermute(block, axis, route)


def mix_forward(state, factors):
    position = lax.axis_index("seq")
    number = lax.axis_size("seq").bit_length() - 1
    for bit_level in range(number):
        partner = swapped(state, "seq", bit_level)
        upper_side = jnp.bitwise_and(jnp.right_shift(position, bit_level), 1) == 1
        own_vals = state.astype(jnp.float32)
        partner_vals = partner.astype(jnp.float32)
        as_lower = factors[bit_level, 0] * own_vals + factors[bit_level, 1] * partner_vals
        as_upper = factors[bit_level, 2] * partner_vals + factors[bit_level, 3] * own_vals
        state = jnp.where(upper_side, as_upper, as_lower).astype(jnp.bfloat16)
    return state


def mix_adjoint(state, factors):
    position = lax.axis_index("seq")
    number = lax.axis_size("seq").bit_length() - 1
    for bit_level in reversed(range(number)):
        partner = swapped(state, "seq", bit_level)
        upper_side = jnp.bitwise_and(jnp.right_shift(position, bit_level), 1) == 1
        own_vals = state.astype(jnp.float32)
        partner_vals = partner.astype(jnp.float32)
        as_lower = factors[bit_level, 0] * own_vals + factors[bit_level, 2] * partner_vals
        as_upper = factors[bit_level, 1] * partner_vals + factors[bit_level, 3] * own_vals
        state = jnp.where(upper_side, as_upper, as_lower).astype(jnp.bfloat16)
    return state


def block_apply(rows, blocks):
    block_len = blocks.shape[0]
    shaped = rows.reshape(-1, block_len, rows.shape[1])
    mixed = jnp.einsum("ij,bjd->bid", blocks, shaped, preferred_element_type=jnp.float32)
    return mixed.reshape(rows.shape).astype(jnp.bfloat16)


def layer_forward(rows, blocks, factors, weights):
    width = rows.shape[1]
    block_width = weights.shape[1]
    nblocks = width // block_width
    blocked = block_apply(rows, blocks)
    state = mix_forward(blocked, factors)
    act = (rows.astype(jnp.float32) + state.astype(jnp.float32)).astype(jnp.bfloat16)
    act3 = act.reshape(-1, nblocks, block_width)
    weight3 = weights.reshape(nblocks, block_width, block_width)
    pre = jnp.einsum("tbi,bio->tbo", act3, weight3, preferred_element_type=jnp.float32)
    return (act3, pre)


def on_device(prev_out, prev_grad, saved_in, seq_mix, coeffs, mixer):
    incoming = from_behind(prev_out, "section", 1)[0]
    upstream = from_behind(prev_grad, "section", -1)[0]
    blocks = seq_mix[0]
    factors = coeffs[0]
    weights = mixer[0]
    rows_dev, width = incoming.shape
    block_width = weights.shape[1]
    nblocks = width // block_width
    block_len = blocks.shape[0]
    act3, pre = layer_forward(incoming, blocks, factors, weights)
    result = (
        (act3.astype(jnp.float32) + jax.nn.silu(pre)).reshape(rows_dev, width).astype(jnp.bfloat16)
    )
    stored = saved_in[0]
    act_two, pre_two = layer_forward(stored, blocks, factors, weights)
    sigma = jax.nn.sigmoid(pre_two)
    gz = (
        upstream.astype(jnp.float32).reshape(-1, nblocks, block_width)
        * (sigma * (1.0 + pre_two * (1.0 - sigma)))
    ).astype(jnp.bfloat16)
    weight3 = weights.reshape(nblocks, block_width, block_width)
    back = jnp.einsum("tbo,bio->tbi", gz, weight3, preferred_element_type=jnp.float32)
    d_act = (upstream.astype(jnp.float32) + back.reshape(rows_dev, width)).astype(jnp.bfloat16)
    weight_term = jnp.einsum(
        "tbi,tbo->bio", act_two, gz, preferred_element_type=jnp.float32
    ).reshape(width, block_width)
    grad_weight = lax.psum_scatter(weight_term, "seq", scatter_dimension=0, tiled=True)
    dblocked = mix_adjoint(d_act, factors)
    dblk = dblocked.reshape(-1, block_len, width)
    stored_blk = stored.reshape(-1, block_len, width)
    block_term = jnp.einsum("bid,bjd->ij", dblk, stored_blk, preferred_element_type=jnp.float32)
    grad_block = lax.psum(block_term, "seq")
    through = jnp.einsum("ij,bid->bjd", blocks, dblk, preferred_element_type=jnp.float32).reshape(
        rows_dev, width
    )
    in_grad = (d_act.astype(jnp.float32) + through).astype(jnp.bfloat16)
    return (result[None], in_grad[None], grad_weight[None], grad_block[None])


def solution(mesh):
    placed = (
        P("section", "seq", None),
        P("section", "seq", None),
        P("section", "seq", None),
        P("section", None, None),
        P("section", None, None, None),
        P("section", None, None),
    )
    return jax.shard_map(
        on_device,
        mesh=mesh,
        in_specs=placed,
        out_specs=(
            P("section", "seq", None),
            P("section", "seq", None),
            P("section", "seq", None),
            P("section", None, None),
        ),
        check_vma=False,
    )
```

profile of v0, /device:TPU:0, one launch (start us, length us, event | category | flops | bytes accessed | tf_op | source)
XLA Modules:
  0.0 301.7 jit_solution(15228928650524788524)
XLA Ops:
  7.2 0.7 copy-done
  7.9 1.3 fusion.1
  9.8 1.3 slice_reduce_fusion.15
  11.2 1.3 fusion.20
  12.6 3.0 collective-permute-start.7
  15.5 10.8 %collective-permute-done.7 = bf16[128,1792]{0,1:T(8,128)(2,1)S(1)} collective-permute-done((bf16[128,1792]{0,1:T(8,128)(2,1)S(1)}, bf16[128,1792]{0,1:T(8,128)(2,1)S(1)}, u32[]{:S(2)}, u32[]{:S(2)}) %collective-permute-start.7) | collective-permute-done | bytes 458784 | tf_op jit(solution)/shard_map/ppermute | solution.py:14
  26.4 1.3 fusion.24
  27.7 1.9 collective-permute-start.8
  29.6 10.3 %collective-permute-done.8 = bf16[128,1792]{0,1:T(8,128)(2,1)S(1)} collective-permute-done((bf16[128,1792]{0,1:T(8,128)(2,1)S(1)}, bf16[128,1792]{0,1:T(8,128)(2,1)S(1)}, u32[]{:S(2)}, u32[]{:S(2)}) %collective-permute-start.8) | collective-permute-done | bytes 458784 | tf_op jit(solution)/shard_map/ppermute | solution.py:14
  39.8 1.3 fusion.28
  41.2 2.6 collective-permute-start.9
  43.7 1.0 copy.12
  44.7 1.5 collective-permute-start.5
  46.2 1.0 copy.13
  47.2 2.8 copy.18
  50.0 13.3 %collective-permute-done.9 = bf16[128,1792]{0,1:T(8,128)(2,1)} collective-permute-done((bf16[128,1792]{0,1:T(8,128)(2,1)S(1)}, bf16[128,1792]{0,1:T(8,128)(2,1)}, u32[]{:S(2)}, u32[]{:S(2)}) %collective-permute-start.9) | collective-permute-done | bytes 458784 | tf_op jit(solution)/shard_map/ppermute | solution.py:14
  63.2 3.0 add_convert_fusion.1
  66.2 0.8 convolution_bitcast_fusion.1
  67.1 0.7 fusion.59
  68.0 0.9 copy-done.4
  69.1 22.5 %collective-permute-done.10 = bf16[128,1792]{0,1:T(8,128)(2,1)S(1)} collective-permute-done((bf16[128,1792]{0,1:T(8,128)(2,1)S(1)}, bf16[128,1792]{0,1:T(8,128)(2,1)S(1)}, u32[]{:S(2)}, u32[]{:S(2)}) %collective-permute-start.10) | collective-permute-done | bytes 458784 | tf_op jit(solution)/shard_map/ppermute | solution.py:14
  91.6 2.2 fusion.36
  93.8 2.0 copy.10
  95.8 0.6 collective-permute-start
  96.4 9.0 %collective-permute-done.11 = bf16[128,1792]{0,1:T(8,128)(2,1)} collective-permute-done((bf16[128,1792]{0,1:T(8,128)(2,1)}, bf16[128,1792]{0,1:T(8,128)(2,1)}, u32[]{:S(2)}, u32[]{:S(2)}) %collective-permute-start.11) | collective-permute-done | bytes 458784 | tf_op jit(solution)/shard_map/ppermute | solution.py:14
  105.5 2.9 fusion.40
  108.8 10.0 %collective-permute-done.12 = bf16[128,1792]{0,1:T(8,128)(2,1)S(1)} collective-permute-done((bf16[128,1792]{0,1:T(8,128)(2,1)S(1)}, bf16[128,1792]{0,1:T(8,128)(2,1)S(1)}, u32[]{:S(2)}, u32[]{:S(2)}) %collective-permute-start.12) | collective-permute-done | bytes 458784 | tf_op jit(solution)/shard_map/ppermute | solution.py:14
  118.8 1.3 fusion.44
  120.3 1.8 collective-permute-done.13
  122.0 2.2 fusion.48
  124.3 0.8 copy-done.2
  125.0 1.0 convolution_bitcast_fusion.3
  126.3 3.7 %fusion.58 = f32[4,448,448]{2,1,0:T(8,128)} fusion(bf16[128,4,448]{0,2,1:T(8,128)(2,1)S(1)} %bitcast.83, f32[128,4,448]{0,2,1:T(8,128)} %copy-done.6, bf16[128,4,448]{0,2,1:T(8,128)(2,1)S(1)} %bitcast.81), kind=kOutput, calls=%fused_computation.135 | convolution fusion | flops 207814656 | bytes 5046272 | tf_op jit(solution)/shard_map/tbi,tbo->bio/dot_general | solution.py:95
  130.0 1.0 copy-done.9
  131.3 12.5 %collective-permute-done.2 = bf16[128,1792]{0,1:T(8,128)(2,1)S(1)} collective-permute-done((bf16[128,1792]{0,1:T(8,128)(2,1)S(1)}, bf16[128,1792]{0,1:T(8,128)(2,1)S(1)}, u32[]{:S(2)}, u32[]{:S(2)}) %collective-permute-start.2) | collective-permute-done | bytes 458784 | tf_op jit(solution)/shard_map/ppermute | solution.py:14
  143.7 1.3 fusion.8
  145.1 0.6 collective-permute-start.3
  146.0 11.1 %collective-permute-done.3 = bf16[128,1792]{0,1:T(8,128)(2,1)S(1)} collective-permute-done((bf16[128,1792]{0,1:T(8,128)(2,1)S(1)}, bf16[128,1792]{0,1:T(8,128)(2,1)S(1)}, u32[]{:S(2)}, u32[]{:S(2)}) %collective-permute-start.3) | collective-permute-done | bytes 458784 | tf_op jit(solution)/shard_map/ppermute | solution.py:14
  157.1 2.2 fusion.12
  159.3 2.6 collective-permute-start.4
  162.1 1.0 copy.17
  163.1 18.6 %collective-permute-done.4 = bf16[128,1792]{0,1:T(8,128)(2,1)} collective-permute-done((bf16[128,1792]{0,1:T(8,128)(2,1)}, bf16[128,1792]{0,1:T(8,128)(2,1)}, u32[]{:S(2)}, u32[]{:S(2)}) %collective-permute-start.4) | collective-permute-done | bytes 458784 | tf_op jit(solution)/shard_map/ppermute | solution.py:14
  181.7 2.9 add_convert_fusion.3
  184.5 0.9 add_convert_fusion.2
  185.4 1.0 copy.16
  186.4 31.9 %all-reduce.2.cloned.1.call-done = f32[1,128,128]{2,1,0:T(8,128)} async-done(((f32[1,128,128]{2,1,0:T(8,128)}), f32[1,128,128]{2,1,0:T(8,128)}) %all-reduce.2.cloned.1.call-update) | async-done | bytes 65552 | tf_op jit(solution)/shard_map/psum | solution.py:103
  218.3 75.1 %reduce-scatter.2.cloned.1.call-done = f32[112,448]{1,0:T(8,128)} async-done(((f32[1792,448]{1,0:T(8,128)}), f32[112,448]{1,0:T(8,128)}) %reduce-scatter.2.cloned.1.call-update) | async-done | bytes 200720 | tf_op jit(solution)/shard_map/reduce_scatter | solution.py:98
  293.4 1.5 copy.20
  (39 shorter events, 2.5 us)
Async XLA Ops:
  7.2 0.8 copy-start
  7.2 211.1 %all-reduce.2.cloned.1.call-start = ((), (), s32[]{:S(2)}) async-start(), calls=%async_computation.2 | async-start | bytes 131072 | tf_op jit(solution)/shard_map/psum | solution.py:103
  9.3 2.0 collective-permute-start.6
  11.2 32.5 %copy-start.11 = (bf16[1,128,1792]{2,1,0:T(8,128)(2,1)S(1)}, bf16[1,128,1792]{2,1,0:T(8,128)(2,1)}, u32[]{:S(2)}) copy-start(bf16[1,128,1792]{2,1,0:T(8,128)(2,1)} %param.7) | copy-start | bytes 1376260
  12.6 13.8 %collective-permute-start.7 = (bf16[128,1792]{0,1:T(8,128)(2,1)S(1)}, bf16[128,1792]{0,1:T(8,128)(2,1)S(1)}, u32[]{:S(2)}, u32[]{:S(2)}) collective-permute-start(bf16[128,1792]{0,1:T(8,128)(2,1)S(1)} %fusion.20), channel_id=1, source_target_pairs={{0,2},{2,0},{1,3},{3,1},{4,6},{6,4},{5,7},{7,5},{8,10},{10,8},{9,1... | collective-permute-start | bytes 1376264 | tf_op jit(solution)/shard_map/ppermute | solution.py:14
  26.3 19.9 %copy-start.1 = (bf16[1,128,1792]{2,1,0:T(8,128)(2,1)S(1)}, bf16[1,128,1792]{2,1,0:T(8,128)(2,1)}, u32[]{:S(2)}) copy-start(bf16[1,128,1792]{2,1,0:T(8,128)(2,1)} %param.8) | copy-start | bytes 1376260
  27.7 12.1 %collective-permute-start.8 = (bf16[128,1792]{0,1:T(8,128)(2,1)S(1)}, bf16[128,1792]{0,1:T(8,128)(2,1)S(1)}, u32[]{:S(2)}, u32[]{:S(2)}) collective-permute-start(bf16[128,1792]{0,1:T(8,128)(2,1)S(1)} %fusion.24), channel_id=1, source_target_pairs={{0,4},{4,0},{1,5},{5,1},{2,6},{6,2},{3,7},{7,3},{8,12},{12,8},{9,1... | collective-permute-start | bytes 1376264 | tf_op jit(solution)/shard_map/ppermute | solution.py:14
  41.2 8.8 %copy-start.10 = (bf16[128,1792]{0,1:T(8,128)(2,1)}, bf16[128,1792]{0,1:T(8,128)(2,1)S(1)}, u32[]{:S(2)}) copy-start(bf16[128,1792]{0,1:T(8,128)(2,1)S(1)} %fusion.28) | copy-start | bytes 1376260
  41.2 22.1 %collective-permute-start.9 = (bf16[128,1792]{0,1:T(8,128)(2,1)S(1)}, bf16[128,1792]{0,1:T(8,128)(2,1)}, u32[]{:S(2)}, u32[]{:S(2)}) collective-permute-start(bf16[128,1792]{0,1:T(8,128)(2,1)S(1)} %fusion.28), channel_id=1, source_target_pairs={{0,8},{8,0},{1,9},{9,1},{2,10},{10,2},{3,11},{11,3},{4,12},{12,4},... | collective-permute-start | bytes 1376264 | tf_op jit(solution)/shard_map/ppermute | solution.py:14
  44.7 22.4 %collective-permute-start.5 = (bf16[1,128,1792]{1,2,0:T(8,128)(2,1)}, bf16[1,128,1792]{1,2,0:T(8,128)(2,1)S(1)}, u32[]{:S(2)}, u32[]{:S(2)}) collective-permute-start(bf16[1,128,1792]{1,2,0:T(8,128)(2,1)} %copy.12), channel_id=1, source_target_pairs={{16,0},{0,16},{17,1},{1,17},{18,2},{2,18},{19,3},{3,19},{20,4},{4,... | collective-permute-start | bytes 1376264 | tf_op jit(solution)/shard_map/ppermute | solution.py:20
  67.1 0.9 copy-start.6
  68.0 0.9 copy-start.4
  69.0 22.6 %collective-permute-start.10 = (bf16[128,1792]{0,1:T(8,128)(2,1)S(1)}, bf16[128,1792]{0,1:T(8,128)(2,1)S(1)}, u32[]{:S(2)}, u32[]{:S(2)}) collective-permute-start(bf16[128,1792]{0,1:T(8,128)(2,1)S(1)} %fusion.50), channel_id=1, source_target_pairs={{0,8},{8,0},{1,9},{9,1},{2,10},{10,2},{3,11},{11,3},{4,12},{12,4},... | collective-permute-start | bytes 1376264 | tf_op jit(solution)/shard_map/ppermute | solution.py:14
  93.8 11.6 %collective-permute-start.11 = (bf16[128,1792]{0,1:T(8,128)(2,1)}, bf16[128,1792]{0,1:T(8,128)(2,1)}, u32[]{:S(2)}, u32[]{:S(2)}) collective-permute-start(bf16[128,1792]{0,1:T(8,128)(2,1)} %fusion.36), channel_id=1, source_target_pairs={{0,4},{4,0},{1,5},{5,1},{2,6},{6,2},{3,7},{7,3},{8,12},{12,8},{9,1... | collective-permute-start | bytes 1376264 | tf_op jit(solution)/shard_map/ppermute | solution.py:14
  95.8 12.6 %collective-permute-start = (bf16[1,128,1792]{1,2,0:T(8,128)(2,1)}, bf16[1,128,1792]{1,2,0:T(8,128)(2,1)S(1)}, u32[]{:S(2)}, u32[]{:S(2)}) collective-permute-start(bf16[1,128,1792]{1,2,0:T(8,128)(2,1)} %copy.10), channel_id=1, source_target_pairs={{16,0},{0,16},{17,1},{1,17},{18,2},{2,18},{19,3},{3,19},{20,4},{4,... | collective-permute-start | bytes 1376264 | tf_op jit(solution)/shard_map/ppermute | solution.py:20
  108.3 10.5 %collective-permute-start.12 = (bf16[128,1792]{0,1:T(8,128)(2,1)S(1)}, bf16[128,1792]{0,1:T(8,128)(2,1)S(1)}, u32[]{:S(2)}, u32[]{:S(2)}) collective-permute-start(bf16[128,1792]{0,1:T(8,128)(2,1)S(1)} %fusion.40), channel_id=1, source_target_pairs={{0,2},{2,0},{1,3},{3,1},{4,6},{6,4},{5,7},{7,5},{8,10},{10,8},{9,1... | collective-permute-start | bytes 1376264 | tf_op jit(solution)/shard_map/ppermute | solution.py:14
  108.4 11.8 %copy-start.7 = (bf16[1,128,1792]{1,2,0:T(8,128)(2,1)}, bf16[1,128,1792]{1,2,0:T(8,128)(2,1)S(1)}, u32[]{:S(2)}) copy-start(bf16[1,128,1792]{1,2,0:T(8,128)(2,1)S(1)} %collective-permute-done) | copy-start | bytes 1376260
  108.7 11.5 %collective-permute-start.1 = (bf16[128,1792]{0,1:T(8,128)(2,1)S(1)}, bf16[128,1792]{0,1:T(8,128)(2,1)S(1)}, u32[]{:S(2)}, u32[]{:S(2)}) collective-permute-start(bf16[128,1792]{0,1:T(8,128)(2,1)S(1)} %fusion), channel_id=1, source_target_pairs={{0,1},{1,0},{2,3},{3,2},{4,5},{5,4},{6,7},{7,6},{8,9},{9,8},{10,11... | collective-permute-start | bytes 1376264 | tf_op jit(solution)/shard_map/ppermute | solution.py:14
  120.2 1.9 collective-permute-start.13
  124.3 0.8 copy-start.2
  126.0 167.3 %reduce-scatter.2.cloned.1.call-start = ((), (), s32[]{:S(2)}) async-start(), calls=%async_computation.1 | async-start | bytes 3899392 | tf_op jit(solution)/shard_map/reduce_scatter | solution.py:98
  129.9 1.0 copy-start.9
  129.9 15.8 %copy-start.3 = (bf16[128,1792]{0,1:T(8,128)(2,1)S(1)}, bf16[128,1792]{0,1:T(8,128)(2,1)}, u32[]{:S(2)}) copy-start(bf16[128,1792]{0,1:T(8,128)(2,1)} %copy-done.2) | copy-start | bytes 1376260
  131.0 31.0 %copy-start.5 = (f32[4,128,448]{1,2,0:T(8,128)S(1)}, f32[4,128,448]{1,2,0:T(8,128)}, u32[]{:S(2)}) copy-start(f32[4,128,448]{1,2,0:T(8,128)} %copy-done.4) | copy-start | bytes 2752516
  131.0 12.8 %collective-permute-start.2 = (bf16[128,1792]{0,1:T(8,128)(2,1)S(1)}, bf16[128,1792]{0,1:T(8,128)(2,1)S(1)}, u32[]{:S(2)}, u32[]{:S(2)}) collective-permute-start(bf16[128,1792]{0,1:T(8,128)(2,1)S(1)} %copy-done.9), channel_id=1, source_target_pairs={{0,2},{2,0},{1,3},{3,1},{4,6},{6,4},{5,7},{7,5},{8,10},{10,8},{9,1... | collective-permute-start | bytes 1376264 | tf_op jit(solution)/shard_map/ppermute | solution.py:14
  145.1 12.0 %collective-permute-start.3 = (bf16[128,1792]{0,1:T(8,128)(2,1)S(1)}, bf16[128,1792]{0,1:T(8,128)(2,1)S(1)}, u32[]{:S(2)}, u32[]{:S(2)}) collective-permute-start(bf16[128,1792]{0,1:T(8,128)(2,1)S(1)} %fusion.8), channel_id=1, source_target_pairs={{0,4},{4,0},{1,5},{5,1},{2,6},{6,2},{3,7},{7,3},{8,12},{12,8},{9,1... | collective-permute-start | bytes 1376264 | tf_op jit(solution)/shard_map/ppermute | solution.py:14
  159.3 22.3 %collective-permute-start.4 = (bf16[128,1792]{0,1:T(8,128)(2,1)}, bf16[128,1792]{0,1:T(8,128)(2,1)}, u32[]{:S(2)}, u32[]{:S(2)}) collective-permute-start(bf16[128,1792]{0,1:T(8,128)(2,1)} %fusion.12), channel_id=1, source_target_pairs={{0,8},{8,0},{1,9},{9,1},{2,10},{10,2},{3,11},{11,3},{4,12},{12,4},... | collective-permute-start | bytes 1376264 | tf_op jit(solution)/shard_map/ppermute | solution.py:14
  161.9 19.7 %copy-start.8 = (bf16[1,128,1792]{1,2,0:T(8,128)(2,1)S(1)}, bf16[1,128,1792]{1,2,0:T(8,128)(2,1)}, u32[]{:S(2)}) copy-start(bf16[1,128,1792]{1,2,0:T(8,128)(2,1)} %copy-done.7) | copy-start | bytes 1376260
Sparse Core Ops, SparseCore 0:
  126.2 92.0 all-reduce.1
  223.2 70.1 reduce-scatter.1
where the time goes:
time: 302 us
  waiting for transfers between devices  227 us (75%)
  other arithmetic  22.3 us (7%)
  local copies, waits for them, and re-layouts  15.1 us (5%)
  between operations  14.3 us (5%)
  starting transfers between devices  14.1 us (5%)
  matrix products  8.92 us (3%)
    ppermute x12, waiting for transfers between devices, swapped(): return lax.ppermute(block, axis, route)  120 us
    reduce_scatter x1, waiting for transfers between devices, on_device(): lax.psum_scatter(weight_term, 'seq', scatter_dimension=0, tiled=True)  75.1 us
    psum x1, waiting for transfers between devices, on_device(): grad_block = lax.psum(block_term, 'seq')  31.9 us
    ppermute x12, starting transfers between devices, swapped(): return lax.ppermute(block, axis, route)  11.7 us
    unnamed x30, local copies, waits for them, and re-layouts  11 us
    convert_element_type x4, other arithmetic, mix_adjoint(): state = jnp.where(upper_side, as_upper, as_lower).astype(jnp.bfloat16)  8.65 us
    convert_element_type x5, other arithmetic, mix_forward(): state = jnp.where(upper_side, as_upper, as_lower).astype(jnp.bfloat16)  7.57 us
  transfers between devices with their start and end apart: 16, of which 13 were waited for; matrix products, arithmetic and copies ran while one was open for 10% of the time, Pallas kernels for 0%

commit v1 on v0

--- a/solution.py
+++ b/solution.py
@@ -100,7 +100,7 @@
     dblk = dblocked.reshape(-1, block_len, width)
     stored_blk = stored.reshape(-1, block_len, width)
     block_term = jnp.einsum("bid,bjd->ij", dblk, stored_blk, preferred_element_type=jnp.float32)
-    grad_block = lax.psum(block_term, "seq")
+    grad_block = jnp.sum(lax.all_gather(block_term, "seq"), axis=0)
     through = jnp.einsum("ij,bid->bjd", blocks, dblk, preferred_element_type=jnp.float32).reshape(
         rows_dev, width
     )

time: 302 us -> 245 us (0.81)
  waiting for transfers between devices: 227 us -> 168 us
    psum x1 -> x0, waiting for transfers between devices: 31.9 us -> none  [on_device(): grad_block = lax.psum(block_term, 'seq')]
    reduce_scatter x1, waiting for transfers between devices: 75.1 us -> 46.1 us  [on_device(): lax.psum_scatter(weight_term, 'seq', scatter_dimension=0, tiled=True)]
    unnamed x30 -> x29, local copies, waits for them, and re-layouts: 11 us -> 9.54 us
  transfers between devices with their start and end apart: 16 -> 16, of which waited for: 13 -> 11; matrix products, arithmetic and copies ran while one was open for 10% -> 13% of each run, Pallas kernels for 0% -> 0%
where the time goes in v1:
time: 245 us; the launch traced here: 244 us
  waiting for transfers between devices  168 us (69%)
  other arithmetic  24.3 us (10%)
  starting transfers between devices  15.1 us (6%)
  between operations  14.3 us (6%)
  local copies, waits for them, and re-layouts  13.7 us (6%)
  matrix products  8.93 us (4%)
    ppermute x12, waiting for transfers between devices, swapped(): return lax.ppermute(block, axis, route)  121 us
    reduce_scatter x1, waiting for transfers between devices, on_device(): lax.psum_scatter(weight_term, 'seq', scatter_dimension=0, tiled=True)  46.1 us
    ppermute x12, starting transfers between devices, swapped(): return lax.ppermute(block, axis, route)  12.7 us
    unnamed x29, local copies, waits for them, and re-layouts  9.54 us
    convert_element_type x4, other arithmetic, mix_adjoint(): state = jnp.where(upper_side, as_upper, as_lower).astype(jnp.bfloat16)  8.65 us
    convert_element_type x5, other arithmetic, mix_forward(): state = jnp.where(upper_side, as_upper, as_lower).astype(jnp.bfloat16)  7.59 us
    convert_element_type x2, other arithmetic, layer_forward(): (rows.astype(jnp.float32) + state.astype(jnp.float32)).astype(jnp.bfloat16)  5.91 us
  transfers between devices with their start and end apart: 16, of which 11 were waited for; matrix products, arithmetic and copies ran while one was open for 13% of the time, Pallas kernels for 0%

profile of v1, /device:TPU:0, one launch (start us, length us, event | category | flops | bytes accessed | tf_op | source)
XLA Modules:
  0.0 243.9 jit_solution(2915484954091573407)
XLA Ops:
  7.2 0.7 copy-done
  7.9 1.3 fusion.1
  9.3 0.5 collective-permute-start.6
  9.8 1.4 slice_reduce_fusion.15
  11.2 1.4 fusion.20
  12.6 2.9 %collective-permute-start.7 = (bf16[128,1792]{0,1:T(8,128)(2,1)S(1)}, bf16[128,1792]{0,1:T(8,128)(2,1)S(1)}, u32[]{:S(2)}, u32[]{:S(2)}) collective-permute-start(bf16[128,1792]{0,1:T(8,128)(2,1)S(1)} %fusion.20), channel_id=1, source_target_pairs={{0,2},{2,0},{1,3},{3,1},{4,6},{6,4},{5,7},{7,5},{8,10},{10,8},{9,1... | collective-permute-start | bytes 1376264 | tf_op jit(solution)/shard_map/ppermute | solution.py:14
  15.5 10.9 %collective-permute-done.7 = bf16[128,1792]{0,1:T(8,128)(2,1)S(1)} collective-permute-done((bf16[128,1792]{0,1:T(8,128)(2,1)S(1)}, bf16[128,1792]{0,1:T(8,128)(2,1)S(1)}, u32[]{:S(2)}, u32[]{:S(2)}) %collective-permute-start.7) | collective-permute-done | bytes 458784 | tf_op jit(solution)/shard_map/ppermute | solution.py:14
  26.4 1.3 fusion.24
  27.7 1.9 collective-permute-start.8
  29.6 10.3 %collective-permute-done.8 = bf16[128,1792]{0,1:T(8,128)(2,1)S(1)} collective-permute-done((bf16[128,1792]{0,1:T(8,128)(2,1)S(1)}, bf16[128,1792]{0,1:T(8,128)(2,1)S(1)}, u32[]{:S(2)}, u32[]{:S(2)}) %collective-permute-start.8) | collective-permute-done | bytes 458784 | tf_op jit(solution)/shard_map/ppermute | solution.py:14
  39.9 1.3 fusion.28
  41.3 2.6 %collective-permute-start.9 = (bf16[128,1792]{0,1:T(8,128)(2,1)S(1)}, bf16[128,1792]{0,1:T(8,128)(2,1)}, u32[]{:S(2)}, u32[]{:S(2)}) collective-permute-start(bf16[128,1792]{0,1:T(8,128)(2,1)S(1)} %fusion.28), channel_id=1, source_target_pairs={{0,8},{8,0},{1,9},{9,1},{2,10},{10,2},{3,11},{11,3},{4,12},{12,4},... | collective-permute-start | bytes 1376264 | tf_op jit(solution)/shard_map/ppermute | solution.py:14
  43.8 1.0 copy.12
  44.8 1.5 collective-permute-start.5
  46.3 1.0 copy.13
  47.3 2.8 %copy.18 = bf16[1,1792,448]{2,1,0:T(8,128)(2,1)S(1)} copy(bf16[1,1792,448]{1,2,0:T(8,128)(2,1)} %param.11) | data formatting | bytes 3211264 | tf_op jit(solution)/shard_map/reshape;squeeze | solution.py:66
  50.0 13.3 %collective-permute-done.9 = bf16[128,1792]{0,1:T(8,128)(2,1)} collective-permute-done((bf16[128,1792]{0,1:T(8,128)(2,1)S(1)}, bf16[128,1792]{0,1:T(8,128)(2,1)}, u32[]{:S(2)}, u32[]{:S(2)}) %collective-permute-start.9) | collective-permute-done | bytes 458784 | tf_op jit(solution)/shard_map/ppermute | solution.py:14
  63.4 3.0 %add_convert_fusion.1 = bf16[128,1792]{0,1:T(8,128)(2,1)S(1)} fusion(bf16[128,1792]{0,1:T(8,128)(2,1)} %copy-done.10, bf16[128,1792]{0,1:T(8,128)(2,1)} %collective-permute-done.9, bf16[1,128,1792]{1,2,0:T(8,128)(2,1)} %copy.13, f32[1792]{0:T(1024)S(1)} %get-tuple-element.9, f32[1792]{0:T(1024)S(1)} %get-tuple-element.10, f32[1792]{0:T(1024)S(1)} %get-tuple-element.11, ...), kind=kLoop, calls=%fused_computation.109 | loop fusion | flops 3211264 | bytes 1863681 | tf_op jit(solution)/shard_map/convert_element_type | solution.py:64
  66.4 0.8 convolution_bitcast_fusion.1
  67.2 0.7 fusion.60
  68.1 0.9 copy-done.4
  69.3 22.5 %collective-permute-done.10 = bf16[128,1792]{0,1:T(8,128)(2,1)S(1)} collective-permute-done((bf16[128,1792]{0,1:T(8,128)(2,1)S(1)}, bf16[128,1792]{0,1:T(8,128)(2,1)S(1)}, u32[]{:S(2)}, u32[]{:S(2)}) %collective-permute-start.10) | collective-permute-done | bytes 458784 | tf_op jit(solution)/shard_map/ppermute | solution.py:14
  91.8 2.2 fusion.36
  94.0 2.0 copy.10
  96.0 0.6 collective-permute-start
  96.6 9.1 %collective-permute-done.11 = bf16[128,1792]{0,1:T(8,128)(2,1)} collective-permute-done((bf16[128,1792]{0,1:T(8,128)(2,1)}, bf16[128,1792]{0,1:T(8,128)(2,1)}, u32[]{:S(2)}, u32[]{:S(2)}) %collective-permute-start.11) | collective-permute-done | bytes 458784 | tf_op jit(solution)/shard_map/ppermute | solution.py:14
  105.7 2.9 %fusion.40 = bf16[128,1792]{0,1:T(8,128)(2,1)S(1)} fusion(bf16[128,1792]{0,1:T(8,128)(2,1)} %collective-permute-done.11, bf16[128,1792]{0,1:T(8,128)(2,1)} %fusion.36, f32[1792]{0:T(1024)S(1)} %get-tuple-element.12, f32[1792]{0:T(1024)S(1)} %get-tuple-element.13, f32[1792]{0:T(1024)S(1)} %get-tuple-element.14, f32[1792]{0:T(1024)S(1)} %get-tuple-element.23, ...), kind=kLoop, calls=%fused_computation.93 | loop fusion | flops 2293760 | bytes 1404929 | tf_op jit(solution)/shard_map/convert_element_type | solution.py:47
  109.0 10.0 %collective-permute-done.12 = bf16[128,1792]{0,1:T(8,128)(2,1)S(1)} collective-permute-done((bf16[128,1792]{0,1:T(8,128)(2,1)S(1)}, bf16[128,1792]{0,1:T(8,128)(2,1)S(1)}, u32[]{:S(2)}, u32[]{:S(2)}) %collective-permute-start.12) | collective-permute-done | bytes 458784 | tf_op jit(solution)/shard_map/ppermute | solution.py:14
  119.0 1.3 fusion.44
  120.5 1.8 collective-permute-done.13
  122.2 2.2 fusion.48
  124.5 0.8 copy-done.2
  125.2 1.0 fusion.52
  126.5 3.7 %fusion.59 = f32[4,448,448]{2,1,0:T(8,128)} fusion(bf16[128,4,448]{0,2,1:T(8,128)(2,1)S(1)} %bitcast.83, f32[128,4,448]{0,2,1:T(8,128)} %copy-done.6, bf16[128,4,448]{0,2,1:T(8,128)(2,1)S(1)} %bitcast.81), kind=kOutput, calls=%fused_computation.135 | convolution fusion | flops 207814656 | bytes 5046272 | tf_op jit(solution)/shard_map/tbi,tbo->bio/dot_general | solution.py:95
  130.2 1.0 copy-done.9
  131.4 13.0 %collective-permute-done.2 = bf16[128,1792]{0,1:T(8,128)(2,1)S(1)} collective-permute-done((bf16[128,1792]{0,1:T(8,128)(2,1)S(1)}, bf16[128,1792]{0,1:T(8,128)(2,1)S(1)}, u32[]{:S(2)}, u32[]{:S(2)}) %collective-permute-start.2) | collective-permute-done | bytes 458784 | tf_op jit(solution)/shard_map/ppermute | solution.py:14
  144.4 1.3 fusion.8
  145.8 0.6 collective-permute-start.3
  146.7 13.9 %collective-permute-done.3 = bf16[128,1792]{0,1:T(8,128)(2,1)S(1)} collective-permute-done((bf16[128,1792]{0,1:T(8,128)(2,1)S(1)}, bf16[128,1792]{0,1:T(8,128)(2,1)S(1)}, u32[]{:S(2)}, u32[]{:S(2)}) %collective-permute-start.3) | collective-permute-done | bytes 458784 | tf_op jit(solution)/shard_map/ppermute | solution.py:14
  160.6 2.2 fusion.12
  162.8 3.7 %collective-permute-start.4 = (bf16[128,1792]{0,1:T(8,128)(2,1)}, bf16[128,1792]{0,1:T(8,128)(2,1)}, u32[]{:S(2)}, u32[]{:S(2)}) collective-permute-start(bf16[128,1792]{0,1:T(8,128)(2,1)} %fusion.12), channel_id=1, source_target_pairs={{0,8},{8,0},{1,9},{9,1},{2,10},{10,2},{3,11},{11,3},{4,12},{12,4},... | collective-permute-start | bytes 1376264 | tf_op jit(solution)/shard_map/ppermute | solution.py:14
  166.6 1.0 copy.17
  167.6 16.7 %collective-permute-done.4 = bf16[128,1792]{0,1:T(8,128)(2,1)} collective-permute-done((bf16[128,1792]{0,1:T(8,128)(2,1)}, bf16[128,1792]{0,1:T(8,128)(2,1)}, u32[]{:S(2)}, u32[]{:S(2)}) %collective-permute-start.4) | collective-permute-done | bytes 458784 | tf_op jit(solution)/shard_map/ppermute | solution.py:14
  184.3 2.9 %add_convert_fusion.3 = bf16[128,1792]{0,1:T(8,128)(2,1)S(1)} fusion(bf16[128,1792]{0,1:T(8,128)(2,1)} %fusion.12, bf16[128,1792]{0,1:T(8,128)(2,1)} %collective-permute-done.4, bf16[1,128,1792]{1,2,0:T(8,128)(2,1)S(1)} %copy-done.8, f32[1792]{0:T(1024)S(1)} %get-tuple-element.9, f32[1792]{0:T(1024)S(1)} %get-tuple-element.10, ...), kind=kLoop, calls=%fused_computation.111 | loop fusion | flops 3211264 | bytes 1863681 | tf_op jit(solution)/shard_map/convert_element_type | solution.py:64
  187.3 0.9 add_convert_fusion.2
  188.1 1.0 copy.16
  189.1 1.9 reduce_sum.9
  191.0 46.1 %reduce-scatter.2.cloned.1.call-done = f32[112,448]{1,0:T(8,128)} async-done(((f32[1792,448]{1,0:T(8,128)}), f32[112,448]{1,0:T(8,128)}) %reduce-scatter.2.cloned.1.call-update) | async-done | bytes 200720 | tf_op jit(solution)/shard_map/reduce_scatter | solution.py:98
  (39 shorter events, 1.9 us)
Async XLA Ops:
  7.2 0.8 copy-start
  7.2 181.9 %all-gather.3.cloned.1.call-start = ((), (), s32[]{:S(2)}) async-start(), calls=%async_computation.2 | async-start | bytes 1114112 | tf_op jit(solution)/shard_map/all_gather | solution.py:103
  9.3 2.0 collective-permute-start.6
  11.2 32.6 %copy-start.11 = (bf16[1,128,1792]{2,1,0:T(8,128)(2,1)S(1)}, bf16[1,128,1792]{2,1,0:T(8,128)(2,1)}, u32[]{:S(2)}) copy-start(bf16[1,128,1792]{2,1,0:T(8,128)(2,1)} %param.7) | copy-start | bytes 1376260
  12.6 13.8 %collective-permute-start.7 = (bf16[128,1792]{0,1:T(8,128)(2,1)S(1)}, bf16[128,1792]{0,1:T(8,128)(2,1)S(1)}, u32[]{:S(2)}, u32[]{:S(2)}) collective-permute-start(bf16[128,1792]{0,1:T(8,128)(2,1)S(1)} %fusion.20), channel_id=1, source_target_pairs={{0,2},{2,0},{1,3},{3,1},{4,6},{6,4},{5,7},{7,5},{8,10},{10,8},{9,1... | collective-permute-start | bytes 1376264 | tf_op jit(solution)/shard_map/ppermute | solution.py:14
  26.4 19.9 %copy-start.1 = (bf16[1,128,1792]{2,1,0:T(8,128)(2,1)S(1)}, bf16[1,128,1792]{2,1,0:T(8,128)(2,1)}, u32[]{:S(2)}) copy-start(bf16[1,128,1792]{2,1,0:T(8,128)(2,1)} %param.8) | copy-start | bytes 1376260
  27.7 12.2 %collective-permute-start.8 = (bf16[128,1792]{0,1:T(8,128)(2,1)S(1)}, bf16[128,1792]{0,1:T(8,128)(2,1)S(1)}, u32[]{:S(2)}, u32[]{:S(2)}) collective-permute-start(bf16[128,1792]{0,1:T(8,128)(2,1)S(1)} %fusion.24), channel_id=1, source_target_pairs={{0,4},{4,0},{1,5},{5,1},{2,6},{6,2},{3,7},{7,3},{8,12},{12,8},{9,1... | collective-permute-start | bytes 1376264 | tf_op jit(solution)/shard_map/ppermute | solution.py:14
  41.2 8.8 %copy-start.10 = (bf16[128,1792]{0,1:T(8,128)(2,1)}, bf16[128,1792]{0,1:T(8,128)(2,1)S(1)}, u32[]{:S(2)}) copy-start(bf16[128,1792]{0,1:T(8,128)(2,1)S(1)} %fusion.28) | copy-start | bytes 1376260
  41.3 22.1 %collective-permute-start.9 = (bf16[128,1792]{0,1:T(8,128)(2,1)S(1)}, bf16[128,1792]{0,1:T(8,128)(2,1)}, u32[]{:S(2)}, u32[]{:S(2)}) collective-permute-start(bf16[128,1792]{0,1:T(8,128)(2,1)S(1)} %fusion.28), channel_id=1, source_target_pairs={{0,8},{8,0},{1,9},{9,1},{2,10},{10,2},{3,11},{11,3},{4,12},{12,4},... | collective-permute-start | bytes 1376264 | tf_op jit(solution)/shard_map/ppermute | solution.py:14
  44.8 22.4 %collective-permute-start.5 = (bf16[1,128,1792]{1,2,0:T(8,128)(2,1)}, bf16[1,128,1792]{1,2,0:T(8,128)(2,1)S(1)}, u32[]{:S(2)}, u32[]{:S(2)}) collective-permute-start(bf16[1,128,1792]{1,2,0:T(8,128)(2,1)} %copy.12), channel_id=1, source_target_pairs={{16,0},{0,16},{17,1},{1,17},{18,2},{2,18},{19,3},{3,19},{20,4},{4,... | collective-permute-start | bytes 1376264 | tf_op jit(solution)/shard_map/ppermute | solution.py:20
  67.2 0.9 copy-start.6
  68.1 0.9 copy-start.4
  69.2 22.6 %collective-permute-start.10 = (bf16[128,1792]{0,1:T(8,128)(2,1)S(1)}, bf16[128,1792]{0,1:T(8,128)(2,1)S(1)}, u32[]{:S(2)}, u32[]{:S(2)}) collective-permute-start(bf16[128,1792]{0,1:T(8,128)(2,1)S(1)} %fusion.50), channel_id=1, source_target_pairs={{0,8},{8,0},{1,9},{9,1},{2,10},{10,2},{3,11},{11,3},{4,12},{12,4},... | collective-permute-start | bytes 1376264 | tf_op jit(solution)/shard_map/ppermute | solution.py:14
  94.0 11.6 %collective-permute-start.11 = (bf16[128,1792]{0,1:T(8,128)(2,1)}, bf16[128,1792]{0,1:T(8,128)(2,1)}, u32[]{:S(2)}, u32[]{:S(2)}) collective-permute-start(bf16[128,1792]{0,1:T(8,128)(2,1)} %fusion.36), channel_id=1, source_target_pairs={{0,4},{4,0},{1,5},{5,1},{2,6},{6,2},{3,7},{7,3},{8,12},{12,8},{9,1... | collective-permute-start | bytes 1376264 | tf_op jit(solution)/shard_map/ppermute | solution.py:14
  96.0 12.6 %collective-permute-start = (bf16[1,128,1792]{1,2,0:T(8,128)(2,1)}, bf16[1,128,1792]{1,2,0:T(8,128)(2,1)S(1)}, u32[]{:S(2)}, u32[]{:S(2)}) collective-permute-start(bf16[1,128,1792]{1,2,0:T(8,128)(2,1)} %copy.10), channel_id=1, source_target_pairs={{16,0},{0,16},{17,1},{1,17},{18,2},{2,18},{19,3},{3,19},{20,4},{4,... | collective-permute-start | bytes 1376264 | tf_op jit(solution)/shard_map/ppermute | solution.py:20
  108.5 10.5 %collective-permute-start.12 = (bf16[128,1792]{0,1:T(8,128)(2,1)S(1)}, bf16[128,1792]{0,1:T(8,128)(2,1)S(1)}, u32[]{:S(2)}, u32[]{:S(2)}) collective-permute-start(bf16[128,1792]{0,1:T(8,128)(2,1)S(1)} %fusion.40), channel_id=1, source_target_pairs={{0,2},{2,0},{1,3},{3,1},{4,6},{6,4},{5,7},{7,5},{8,10},{10,8},{9,1... | collective-permute-start | bytes 1376264 | tf_op jit(solution)/shard_map/ppermute | solution.py:14
  108.6 11.8 %copy-start.7 = (bf16[1,128,1792]{1,2,0:T(8,128)(2,1)}, bf16[1,128,1792]{1,2,0:T(8,128)(2,1)S(1)}, u32[]{:S(2)}) copy-start(bf16[1,128,1792]{1,2,0:T(8,128)(2,1)S(1)} %collective-permute-done) | copy-start | bytes 1376260
  108.9 11.5 %collective-permute-start.1 = (bf16[128,1792]{0,1:T(8,128)(2,1)S(1)}, bf16[128,1792]{0,1:T(8,128)(2,1)S(1)}, u32[]{:S(2)}, u32[]{:S(2)}) collective-permute-start(bf16[128,1792]{0,1:T(8,128)(2,1)S(1)} %fusion), channel_id=1, source_target_pairs={{0,1},{1,0},{2,3},{3,2},{4,5},{5,4},{6,7},{7,6},{8,9},{9,8},{10,11... | collective-permute-start | bytes 1376264 | tf_op jit(solution)/shard_map/ppermute | solution.py:14
  120.4 1.9 collective-permute-start.13
  124.5 0.8 copy-start.2
  126.2 110.9 %reduce-scatter.2.cloned.1.call-start = ((), (), s32[]{:S(2)}) async-start(), calls=%async_computation.1 | async-start | bytes 3899392 | tf_op jit(solution)/shard_map/reduce_scatter | solution.py:98
  130.1 1.0 copy-start.9
  130.1 16.3 %copy-start.3 = (bf16[128,1792]{0,1:T(8,128)(2,1)S(1)}, bf16[128,1792]{0,1:T(8,128)(2,1)}, u32[]{:S(2)}) copy-start(bf16[128,1792]{0,1:T(8,128)(2,1)} %copy-done.2) | copy-start | bytes 1376260
  131.2 35.3 %copy-start.5 = (f32[4,128,448]{1,2,0:T(8,128)S(1)}, f32[4,128,448]{1,2,0:T(8,128)}, u32[]{:S(2)}) copy-start(f32[4,128,448]{1,2,0:T(8,128)} %copy-done.4) | copy-start | bytes 2752516
  131.2 13.3 %collective-permute-start.2 = (bf16[128,1792]{0,1:T(8,128)(2,1)S(1)}, bf16[128,1792]{0,1:T(8,128)(2,1)S(1)}, u32[]{:S(2)}, u32[]{:S(2)}) collective-permute-start(bf16[128,1792]{0,1:T(8,128)(2,1)S(1)} %copy-done.9), channel_id=1, source_target_pairs={{0,2},{2,0},{1,3},{3,1},{4,6},{6,4},{5,7},{7,5},{8,10},{10,8},{9,1... | collective-permute-start | bytes 1376264 | tf_op jit(solution)/shard_map/ppermute | solution.py:14
  145.8 14.8 %collective-permute-start.3 = (bf16[128,1792]{0,1:T(8,128)(2,1)S(1)}, bf16[128,1792]{0,1:T(8,128)(2,1)S(1)}, u32[]{:S(2)}, u32[]{:S(2)}) collective-permute-start(bf16[128,1792]{0,1:T(8,128)(2,1)S(1)} %fusion.8), channel_id=1, source_target_pairs={{0,4},{4,0},{1,5},{5,1},{2,6},{6,2},{3,7},{7,3},{8,12},{12,8},{9,1... | collective-permute-start | bytes 1376264 | tf_op jit(solution)/shard_map/ppermute | solution.py:14
  162.8 21.6 %collective-permute-start.4 = (bf16[128,1792]{0,1:T(8,128)(2,1)}, bf16[128,1792]{0,1:T(8,128)(2,1)}, u32[]{:S(2)}, u32[]{:S(2)}) collective-permute-start(bf16[128,1792]{0,1:T(8,128)(2,1)} %fusion.12), channel_id=1, source_target_pairs={{0,8},{8,0},{1,9},{9,1},{2,10},{10,2},{3,11},{11,3},{4,12},{12,4},... | collective-permute-start | bytes 1376264 | tf_op jit(solution)/shard_map/ppermute | solution.py:14
  166.5 17.9 %copy-start.8 = (bf16[1,128,1792]{1,2,0:T(8,128)(2,1)S(1)}, bf16[1,128,1792]{1,2,0:T(8,128)(2,1)}, u32[]{:S(2)}) copy-start(bf16[1,128,1792]{1,2,0:T(8,128)(2,1)} %copy-done.7) | copy-start | bytes 1376260
Sparse Core Ops, SparseCore 0:
  126.3 38.7 all-gather.2
  169.5 67.5 reduce-scatter.1
